TPU v7x, 512 devices: a whole 4x8x8 slice. The times are simulated.
512 devices in a mesh: wide: 64 (over z, x, core), narrow: 8 (over y).
Axes of the slice: x: 4, y: 8, z: 8, core: 2. Of those that a mesh axis runs over, the one named last changes fastest.
Arguments:
- charges: float32 [64, 1048576], P(None, ('wide', 'narrow')), may hold values from -6 to 6
- leaf_angle: float32 [64, 65536], P(None, ('wide', 'narrow')), may hold values from -3.140625 to 3.140625
- lagrange: float32 [48, 64], replicated, may hold values from -0.75 to 0.75
- level_angle: float32 [2, 48, 65536], P(None, None, ('wide', 'narrow')), may hold values from -3.140625 to 3.140625
- level_self: float32 [2, 96, 96], replicated, may hold values from -0.4375 to 0.4375
- level_peer: float32 [2, 96, 96], replicated, may hold values from -0.4375 to 0.4375
- switch_angle: float32 [48, 65536], P(None, ('wide', 'narrow')), may hold values from -3.140625 to 3.140625
- switch_matrix: float32 [96, 96], replicated, may hold values from -0.625 to 0.625
- out_angle: float32 [64, 65536], P(None, ('wide', 'narrow')), may hold values from -3.140625 to 3.140625
- evaluate: float32 [64, 48], replicated, may hold values from -0.875 to 0.875
Outputs:
- field: bfloat16 [64, 1048576], P(None, ('wide', 'narrow'))
All inputs are finite; a program needn't handle non-finite values.
Results may differ from a plain program's by a relative error of at most 0.0049.
Values may be sent and summed in bfloat16 or wider, within the bound.
No kernel may reach another device: no remote copies, remote signals or barrier semaphores. Data moves between devices by JAX's collectives and lax.ppermute only.
A program may use at most 64 MiB of HBM per device.

v0:
```python
import jax
import jax.numpy as jnp
from jax import lax
from jax.sharding import PartitionSpec as P


def from_partner(value, axis, apart):
    mask = 2**apart
    pairs = [(source, source ^ mask) for source in range(lax.axis_size(axis))]
    return lax.ppermute(value, axis, pairs)


def product(left, right):
    return jnp.dot(left, right, precision=lax.Precision.HIGHEST, preferred_element_type=jnp.float32)


def rotate(boxes_state, phase_angle, per_box):
    rank = phase_angle.shape[0]
    cos_part = jnp.repeat(jnp.cos(phase_angle), per_box, axis=1)
    sin_part = jnp.repeat(jnp.sin(phase_angle), per_box, axis=1)
    real_part = boxes_state[:rank]
    imag_part = boxes_state[rank:]
    return jnp.concatenate(
        [cos_part * real_part - sin_part * imag_part, sin_part * real_part + cos_part * imag_part],
        axis=0,
    )


def butterfly_level(boxes_state, self_matrix, peer_matrix, phase_angle, bit, per_box):
    sent_state = boxes_state.astype(jnp.bfloat16)
    received = from_partner(sent_state, "narrow", bit)
    combined = product(self_matrix, boxes_state) + product(
        peer_matrix, received.astype(jnp.float32)
    )
    return rotate(combined, phase_angle, per_box)


def leaf_weights(lagrange, point_charges, point_angle, per_box):
    cos_leaf = jnp.repeat(jnp.cos(point_angle), per_box, axis=1)
    sin_leaf = jnp.repeat(jnp.sin(point_angle), per_box, axis=1)
    return jnp.concatenate(
        [product(lagrange, cos_leaf * point_charges), product(lagrange, sin_leaf * point_charges)],
        axis=0,
    )


def body(
    charges,
    leaf_angle,
    lagrange,
    level_angle,
    level_self,
    level_peer,
    switch_angle,
    switch_matrix,
    out_angle,
    evaluate,
):
    per_box = charges.shape[1] // leaf_angle.shape[1]
    rank = lagrange.shape[0]
    last_bit = lax.axis_size("narrow").bit_length() - 2
    boxes_state = leaf_weights(lagrange, charges, leaf_angle, per_box)
    boxes_state = butterfly_level(
        boxes_state, level_self[0], level_peer[0], level_angle[0], 0, per_box
    )
    boxes_state = lax.all_to_all(boxes_state, "wide", split_axis=1, concat_axis=1, tiled=True)
    boxes_state = rotate(product(switch_matrix, boxes_state), switch_angle, per_box)
    boxes_state = butterfly_level(
        boxes_state, level_self[1], level_peer[1], level_angle[1], last_bit, per_box
    )
    real_part = product(evaluate, boxes_state[:rank])
    imag_part = product(evaluate, boxes_state[rank:])
    cos_out = jnp.repeat(jnp.cos(out_angle), per_box, axis=1)
    sin_out = jnp.repeat(jnp.sin(out_angle), per_box, axis=1)
    return (cos_out * real_part - sin_out * imag_part).astype(jnp.bfloat16)


def solution(mesh):
    return jax.shard_map(
        body,
        mesh=mesh,
        in_specs=(
            P(None, ("wide", "narrow")),
            P(None, ("wide", "narrow")),
            P(),
            P(None, None, ("wide", "narrow")),
            P(),
            P(),
            P(None, ("wide", "narrow")),
            P(),
            P(None, ("wide", "narrow")),
            P(),
        ),
        out_specs=P(None, ("wide", "narrow")),
        check_vma=False,
    )
```

profile of v0, /device:TPU:17, one launch (start us, length us, event | category | flops | bytes accessed | tf_op | source)
XLA Modules:
  0.0 94.2 jit_solution(16708297158461650053)
XLA Ops:
  0.0 0.9 fusion.31
  1.1 1.4 %copy.16 = f32[64,2048]{0,1:T(8,128)S(1)} copy(f32[64,2048]{1,0:T(8,128)} %param.10) | data formatting | bytes 1048576 | tf_op args[0]
  2.6 0.6 copy-done.9
  3.2 1.3 %convolution_bitcast_fusion.3 = f32[48,2048]{1,0:T(8,128)S(1)} fusion(f32[64,2048]{0,1:T(8,128)S(1)} %get-tuple-element.10, f32[48,64]{1,0:T(8,128)S(1)} %copy-done.9), kind=kOutput, calls=%fused_computation.11 | convolution fusion | flops 75497472 | bytes 929792 | tf_op jit(solution)/shard_map/dot_general | solution.py:14
  4.5 1.3 %convolution_bitcast_fusion.4 = f32[48,2048]{1,0:T(8,128)S(1)} fusion(f32[64,2048]{0,1:T(8,128)S(1)} %get-tuple-element.9, f32[48,64]{1,0:T(8,128)S(1)} %copy-done.9), kind=kOutput, calls=%fused_computation.12 | convolution fusion | flops 75497472 | bytes 929792 | tf_op jit(solution)/shard_map/dot_general | solution.py:14
  5.8 3.2 %collective-permute-start = (bf16[96,2048]{1,0:T(8,128)(2,1)S(1)}, bf16[96,2048]{1,0:T(8,128)(2,1)S(1)}, u32[]{:S(2)}, u32[]{:S(2)}) collective-permute-start(bf16[96,2048]{1,0:T(8,128)(2,1)S(1)} %fusion.8), channel_id=1, source_target_pairs={{0,1},{1,0},{2,3},{3,2},{4,5},{5,4},{6,7},{7,6},{8,9},{9,8},{10,11... | collective-permute-start | bytes 1179656 | tf_op jit(solution)/shard_map/ppermute | solution.py:10
  9.0 0.8 sine_bitcast_fusion.1
  10.0 0.3 copy.19
  10.5 0.3 copy.21
  10.8 0.6 copy-done.4
  11.4 0.8 fusion.9
  12.3 5.4 %collective-permute-done = bf16[96,2048]{1,0:T(8,128)(2,1)S(1)} collective-permute-done((bf16[96,2048]{1,0:T(8,128)(2,1)S(1)}, bf16[96,2048]{1,0:T(8,128)(2,1)S(1)}, u32[]{:S(2)}, u32[]{:S(2)}) %collective-permute-start) | collective-permute-done | bytes 393248 | tf_op jit(solution)/shard_map/ppermute | solution.py:10
  17.7 0.5 fusion.1
  18.3 1.3 %copy.24 = f32[96,2048]{0,1:T(8,128)} copy(f32[96,2048]{1,0:T(8,128)S(1)} %pad_maximum_fusion.1) | data formatting | bytes 1572864 | tf_op jit(solution)/shard_map/concatenate | solution.py:23
  19.7 15.0 %all-to-all-start = ((f32[96,64,32]{0,2,1:T(8,128)}), f32[96,64,32]{0,2,1:T(8,128)S(1)}, u32[]{:S(2)}, u32[]{:S(2)}) async-start(f32[96,64,32]{0,2,1:T(8,128)} %bitcast.15), calls=%async_computation | async-start | bytes 2097152 | tf_op jit(solution)/shard_map/all_to_all | solution.py:66
  35.0 0.3 copy.25
  35.5 1.1 %copy.27 = f32[48,2048]{1,0:T(8,128)} copy(f32[48,2048]{0,1:T(8,128)S(1)} %bitcast.70) | data formatting | bytes 786432 | tf_op jit(solution)/shard_map/reshape | solution.py:20
  36.8 0.3 copy.30
  37.1 0.4 copy-done.5
  37.7 0.3 copy.32
  38.0 24.7 %all-to-all-done = f32[96,64,32]{0,2,1:T(8,128)S(1)} async-done(((f32[96,64,32]{0,2,1:T(8,128)}), f32[96,64,32]{0,2,1:T(8,128)S(1)}, u32[]{:S(2)}, u32[]{:S(2)}) %all-to-all-start) | async-done | bytes 786464 | tf_op jit(solution)/shard_map/all_to_all | solution.py:66
  62.7 1.2 %convolution_bitcast_fusion = f32[96,2048]{1,0:T(8,128)S(1)} fusion(f32[96,2048]{0,1:T(8,128)S(1)} %bitcast.66, f32[96,96]{1,0:T(8,128)S(1)} %copy-done), kind=kOutput, calls=%fused_computation | convolution fusion | flops 226492416 | bytes 1609728 | tf_op jit(solution)/shard_map/dot_general | solution.py:14
  64.0 0.8 fusion.6
  64.8 5.8 %collective-permute-start.1 = (bf16[96,2048]{1,0:T(8,128)(2,1)}, bf16[96,2048]{1,0:T(8,128)(2,1)}, u32[]{:S(2)}, u32[]{:S(2)}) collective-permute-start(bf16[96,2048]{1,0:T(8,128)(2,1)} %fusion.6), channel_id=1, source_target_pairs={{0,4},{1,5},{2,6},{3,7},{4,0},{5,1},{6,2},{7,3},{8,12},{9,13},{10,... | collective-permute-start | bytes 1179656 | tf_op jit(solution)/shard_map/ppermute | solution.py:10
  71.0 0.3 copy.33
  71.5 1.1 %copy.37 = f32[64,2048]{1,0:T(8,128)} copy(f32[64,2048]{0,1:T(8,128)S(1)} %bitcast.74) | data formatting | bytes 1048576 | tf_op jit(solution)/shard_map/reshape | solution.py:74
  72.6 0.8 fusion.7
  73.5 16.9 %collective-permute-done.1 = bf16[96,2048]{1,0:T(8,128)(2,1)} collective-permute-done((bf16[96,2048]{1,0:T(8,128)(2,1)}, bf16[96,2048]{1,0:T(8,128)(2,1)}, u32[]{:S(2)}, u32[]{:S(2)}) %collective-permute-start.1) | collective-permute-done | bytes 393248 | tf_op jit(solution)/shard_map/ppermute | solution.py:10
  90.4 1.5 %fusion = f32[96,2048]{1,0:T(8,128)S(1)} fusion(f32[2048,96]{0,1:T(8,128)S(1)} %fusion.7, bf16[96,2048]{1,0:T(8,128)(2,1)} %collective-permute-done.1, f32[2,96,96]{2,1,0:T(8,128)S(1)} %copy-done.8), kind=kOutput, calls=%fused_computation.2 | convolution fusion | flops 226689024 | bytes 2015232 | tf_op jit(solution)/shard_map/dot_general | solution.py:14
  91.9 0.6 fusion.4
  92.5 0.4 copy-done.1
  92.9 1.3 %fusion.5 = bf16[64,2048]{1,0:T(8,128)(2,1)} fusion(f32[64,2048]{1,0:T(8,128)S(1)} %fusion.4, f32[64,2048]{1,0:T(8,128)S(1)} %copy-done.1, f32[64,48]{0,1:T(8,128)S(1)} %copy-done.3, f32[48,2048]{1,0:T(8,128)S(1)} %copy.30, f32[48,2048]{1,0:T(8,128)S(1)} %copy.32, f32[96,2048]{1,0:T(8,128)S(1)} %fusion), kind=kOutput, calls=%fused_computation.10 | convolution fusion | flops 76185600 | bytes 2895872 | tf_op jit(solution)/shard_map/dot_general | solution.py:14
  (47 shorter events, 2.2 us)
Async XLA Ops:
  0.0 62.7 %copy-start = (f32[96,96]{1,0:T(8,128)S(1)}, f32[96,96]{1,0:T(8,128)}, u32[]{:S(2)}) copy-start(f32[96,96]{1,0:T(8,128)} %param.17) | copy-start | bytes 110596
  2.5 0.7 copy-start.9
  5.8 3.3 %copy-start.10 = (f32[2,48,128]{2,1,0:T(8,128)S(1)}, f32[2,48,128]{2,1,0:T(8,128)}, u32[]{:S(2)}) copy-start(f32[2,48,128]{2,1,0:T(8,128)} %param.13) | copy-start | bytes 147460
  5.8 11.9 %collective-permute-start = (bf16[96,2048]{1,0:T(8,128)(2,1)S(1)}, bf16[96,2048]{1,0:T(8,128)(2,1)S(1)}, u32[]{:S(2)}, u32[]{:S(2)}) collective-permute-start(bf16[96,2048]{1,0:T(8,128)(2,1)S(1)} %fusion.8), channel_id=1, source_target_pairs={{0,1},{1,0},{2,3},{3,2},{4,5},{5,4},{6,7},{7,6},{8,9},{9,8},{10,11... | collective-permute-start | bytes 1179656 | tf_op jit(solution)/shard_map/ppermute | solution.py:10
  10.5 0.9 copy-start.4
  11.4 6.3 %copy-start.7 = (f32[2,96,96]{2,1,0:T(8,128)S(1)}, f32[2,96,96]{2,1,0:T(8,128)}, u32[]{:S(2)}) copy-start(f32[2,96,96]{2,1,0:T(8,128)} %param.15) | copy-start | bytes 221188
  19.7 15.0 %copy-start.12 = (f32[48,128]{1,0:T(8,128)S(1)}, f32[48,128]{1,0:T(8,128)}, u32[]{:S(2)}) copy-start(f32[48,128]{1,0:T(8,128)} %param.16) | copy-start | bytes 73732
  19.7 43.0 %all-to-all-start = ((f32[96,64,32]{0,2,1:T(8,128)}), f32[96,64,32]{0,2,1:T(8,128)S(1)}, u32[]{:S(2)}, u32[]{:S(2)}) async-start(f32[96,64,32]{0,2,1:T(8,128)} %bitcast.15), calls=%async_computation | async-start | bytes 2097152 | tf_op jit(solution)/shard_map/all_to_all | solution.py:66
  35.5 1.1 %copy-start.6 = (f32[48,128]{1,0:T(8,128)S(1)}, f32[48,128]{1,0:T(8,128)}, u32[]{:S(2)}) copy-start(f32[48,128]{1,0:T(8,128)} %get-tuple-element.14) | copy-start | bytes 73732
  36.7 0.7 copy-start.5
  62.7 1.2 %copy-start.2 = (f32[48,2048]{1,0:T(8,128)S(1)}, f32[48,2048]{1,0:T(8,128)}, u32[]{:S(2)}) copy-start(f32[48,2048]{1,0:T(8,128)} %copy.27) | copy-start | bytes 1179652
  64.0 6.7 %copy-start.11 = (f32[64,128]{1,0:T(8,128)S(1)}, f32[64,128]{1,0:T(8,128)}, u32[]{:S(2)}) copy-start(f32[64,128]{1,0:T(8,128)} %param.18) | copy-start | bytes 98308
  64.8 25.5 %collective-permute-start.1 = (bf16[96,2048]{1,0:T(8,128)(2,1)}, bf16[96,2048]{1,0:T(8,128)(2,1)}, u32[]{:S(2)}, u32[]{:S(2)}) collective-permute-start(bf16[96,2048]{1,0:T(8,128)(2,1)} %fusion.6), channel_id=1, source_target_pairs={{0,4},{1,5},{2,6},{3,7},{4,0},{5,1},{6,2},{7,3},{8,12},{9,13},{10,... | collective-permute-start | bytes 1179656 | tf_op jit(solution)/shard_map/ppermute | solution.py:10
  72.6 17.8 %copy-start.8 = (f32[2,96,96]{2,1,0:T(8,128)S(1)}, f32[2,96,96]{2,1,0:T(8,128)}, u32[]{:S(2)}) copy-start(f32[2,96,96]{2,1,0:T(8,128)} %param.15) | copy-start | bytes 221188
  73.5 18.4 %copy-start.3 = (f32[64,48]{0,1:T(8,128)S(1)}, f32[64,48]{0,1:T(8,128)}, u32[]{:S(2)}) copy-start(f32[64,48]{0,1:T(8,128)} %param.19) | copy-start | bytes 36868
  91.9 1.0 %copy-start.1 = (f32[64,2048]{1,0:T(8,128)S(1)}, f32[64,2048]{1,0:T(8,128)}, u32[]{:S(2)}) copy-start(f32[64,2048]{1,0:T(8,128)} %copy.37) | copy-start | bytes 1572868
where the time goes:
time: 94.9 us; the launch traced here: 94.2 us
  waiting for transfers between devices  47.1 us (50%)
  starting transfers between devices  24 us (25%)
  local copies, waits for them, and re-layouts  12.2 us (13%)
  matrix products  9.29 us (10%)
  other arithmetic  1.23 us (1%)
    all_to_all x1, waiting for transfers between devices, body(): lax.all_to_all(boxes_state, 'wide', split_axis=1, concat_axis=1, tiled=True)  24.7 us
    ppermute x2, waiting for transfers between devices, from_partner(): return lax.ppermute(value, axis, pairs)  22.4 us
    all_to_all x1, starting transfers between devices, body(): lax.all_to_all(boxes_state, 'wide', split_axis=1, concat_axis=1, tiled=True)  15 us
    dot_general x9, matrix products, product(): jnp.dot(left, right, precision=lax.Precision.HIGHEST, preferred_element_t...  9.29 us
    ppermute x2, starting transfers between devices, from_partner(): return lax.ppermute(value, axis, pairs)  9.03 us
    unnamed x27, local copies, waits for them, and re-layouts  3.41 us
  transfers between devices with their start and end apart: 3, of which 3 were waited for; matrix products, arithmetic and copies ran while one was open for 9% of the time, Pallas kernels for 0%

commit v1 on v0

--- a/solution.py
+++ b/solution.py
@@ -63,7 +63,12 @@
     boxes_state = butterfly_level(
         boxes_state, level_self[0], level_peer[0], level_angle[0], 0, per_box
     )
-    boxes_state = lax.all_to_all(boxes_state, "wide", split_axis=1, concat_axis=1, tiled=True)
+    boxes_state = jnp.concatenate(
+        lax.all_to_all(
+            jnp.stack(jnp.split(boxes_state, lax.axis_size("wide"), axis=1)), "wide", 0, 0
+        ),
+        axis=1,
+    )
     boxes_state = rotate(product(switch_matrix, boxes_state), switch_angle, per_box)
     boxes_state = butterfly_level(
         boxes_state, level_self[1], level_peer[1], level_angle[1], last_bit, per_box

time: 94.9 us -> 138 us (1.45)
  local copies, waits for them, and re-layouts: 12.2 us -> 54.1 us
    unnamed x27 -> x90, local copies, waits for them, and re-layouts: 3.41 us -> 41.3 us
    another operation x0 -> x65, local copies, waits for them, and re-layouts: none -> 5.38 us  [body(): jnp.stack(jnp.split(boxes_state, lax.axis_size('wide'), axis=1))]
  transfers between devices with their start and end apart: 3 -> 3, of which waited for: 3 -> 3; matrix products, arithmetic and copies ran while one was open for 9% -> 6% of each run, Pallas kernels for 0% -> 0%
where the time goes in v1:
time: 138 us; the launch traced here: 137 us
  local copies, waits for them, and re-layouts  54.1 us (39%)
  waiting for transfers between devices  47.1 us (34%)
  starting transfers between devices  24 us (17%)
  matrix products  9.28 us (7%)
  other arithmetic  2.22 us (2%)
    unnamed x90, local copies, waits for them, and re-layouts  41.3 us
    all_to_all x1, waiting for transfers between devices, body(): lax.all_to_all(jnp.stack(jnp.split(boxes_state, lax.axis_size('wide'), ax...  24.7 us
    ppermute x2, waiting for transfers between devices, from_partner(): return lax.ppermute(value, axis, pairs)  22.3 us
    all_to_all x1, starting transfers between devices, body(): lax.all_to_all(jnp.stack(jnp.split(boxes_state, lax.axis_size('wide'), ax...  15 us
    dot_general x9, matrix products, product(): jnp.dot(left, right, precision=lax.Precision.HIGHEST, preferred_element_t...  9.28 us
    ppermute x2, starting transfers between devices, from_partner(): return lax.ppermute(value, axis, pairs)  9.03 us
    another operation x65, local copies, waits for them, and re-layouts, body(): jnp.stack(jnp.split(boxes_state, lax.axis_size('wide'), axis=1))  5.38 us
  transfers between devices with their start and end apart: 3, of which 3 were waited for; matrix products, arithmetic and copies ran while one was open for 6% of the time, Pallas kernels for 0%

profile of v1, /device:TPU:17, one launch (start us, length us, event | category | flops | bytes accessed | tf_op | source)
XLA Modules:
  0.0 137.2 jit_solution(1930056417350603433)
XLA Ops:
  0.0 0.9 fusion.158
  1.1 1.4 %copy.43 = f32[64,2048]{0,1:T(8,128)S(1)} copy(f32[64,2048]{1,0:T(8,128)} %param.10) | data formatting | bytes 1048576 | tf_op args[0]
  3.2 1.3 convolution_bitcast_fusion.3
  4.5 1.3 convolution_bitcast_fusion.4
  5.8 3.2 %collective-permute-start = (bf16[96,2048]{1,0:T(8,128)(2,1)S(1)}, bf16[96,2048]{1,0:T(8,128)(2,1)S(1)}, u32[]{:S(2)}, u32[]{:S(2)}) collective-permute-start(bf16[96,2048]{1,0:T(8,128)(2,1)S(1)} %fusion.8), channel_id=1, source_target_pairs={{0,1},{1,0},{2,3},{3,2},{4,5},{5,4},{6,7},{7,6},{8,9},{9,8},{10,11... | collective-permute-start | bytes 1179656 | tf_op jit(solution)/shard_map/ppermute | solution.py:10
  9.0 0.8 sine_bitcast_fusion.1
  11.4 0.8 fusion.9
  12.3 5.4 %collective-permute-done = bf16[96,2048]{1,0:T(8,128)(2,1)S(1)} collective-permute-done((bf16[96,2048]{1,0:T(8,128)(2,1)S(1)}, bf16[96,2048]{1,0:T(8,128)(2,1)S(1)}, u32[]{:S(2)}, u32[]{:S(2)}) %collective-permute-start) | collective-permute-done | bytes 393248 | tf_op jit(solution)/shard_map/ppermute | solution.py:10
  19.4 0.6 constant_dynamic-update-slice_fusion.63
  24.8 0.6 constant_dynamic-update-slice_fusion.62
  26.0 0.6 constant_dynamic-update-slice_fusion.60
  31.4 0.6 constant_dynamic-update-slice_fusion.51
  42.2 0.6 constant_dynamic-update-slice_fusion.33
  42.9 0.6 constant_dynamic-update-slice_fusion.32
  46.5 0.6 constant_dynamic-update-slice_fusion.26
  47.7 0.6 constant_dynamic-update-slice_fusion.24
  50.7 0.6 constant_dynamic-update-slice_fusion.19
  52.5 0.6 constant_dynamic-update-slice_fusion.16
  60.3 0.6 constant_dynamic-update-slice_fusion.3
  62.1 0.6 constant_dynamic-update-slice_fusion
  62.7 15.0 %all-to-all-start = ((f32[64,96,32]{1,2,0:T(8,128)}), f32[64,96,32]{1,2,0:T(8,128)S(1)}, u32[]{:S(2)}, u32[]{:S(2)}) async-start(f32[64,96,32]{1,2,0:T(8,128)} %constant_dynamic-update-slice_fusion), calls=%async_computation | async-start | bytes 2097152 | tf_op jit(solution)/shard_map/all_to_all | solution.py:67
  78.5 1.1 copy.117
  81.0 24.7 %all-to-all-done = f32[64,96,32]{1,2,0:T(8,128)S(1)} async-done(((f32[64,96,32]{1,2,0:T(8,128)}), f32[64,96,32]{1,2,0:T(8,128)S(1)}, u32[]{:S(2)}, u32[]{:S(2)}) %all-to-all-start) | async-done | bytes 786464 | tf_op jit(solution)/shard_map/all_to_all | solution.py:67
  105.7 1.2 convolution_bitcast_fusion
  107.1 0.8 fusion.6
  107.9 5.8 %collective-permute-start.1 = (bf16[96,2048]{1,0:T(8,128)(2,1)}, bf16[96,2048]{1,0:T(8,128)(2,1)}, u32[]{:S(2)}, u32[]{:S(2)}) collective-permute-start(bf16[96,2048]{1,0:T(8,128)(2,1)} %fusion.6), channel_id=1, source_target_pairs={{0,4},{1,5},{2,6},{3,7},{4,0},{5,1},{6,2},{7,3},{8,12},{9,13},{10,... | collective-permute-start | bytes 1179656 | tf_op jit(solution)/shard_map/ppermute | solution.py:10
  114.5 1.1 copy.127
  115.7 0.8 fusion.7
  116.5 16.9 %collective-permute-done.1 = bf16[96,2048]{1,0:T(8,128)(2,1)} collective-permute-done((bf16[96,2048]{1,0:T(8,128)(2,1)}, bf16[96,2048]{1,0:T(8,128)(2,1)}, u32[]{:S(2)}, u32[]{:S(2)}) %collective-permute-start.1) | collective-permute-done | bytes 393248 | tf_op jit(solution)/shard_map/ppermute | solution.py:10
  133.4 1.4 %fusion = f32[96,2048]{1,0:T(8,128)S(1)} fusion(f32[2048,96]{0,1:T(8,128)S(1)} %fusion.7, bf16[96,2048]{1,0:T(8,128)(2,1)} %collective-permute-done.1, f32[2,96,96]{2,1,0:T(8,128)S(1)} %copy-done.8), kind=kOutput, calls=%fused_computation.128 | convolution fusion | flops 226689024 | bytes 2015232 | tf_op jit(solution)/shard_map/dot_general | solution.py:14
  134.9 0.6 fusion.4
  135.9 1.3 fusion.5
  (181 shorter events, 43.4 us)
Async XLA Ops:
  0.0 105.7 %copy-start = (f32[96,96]{1,0:T(8,128)S(1)}, f32[96,96]{1,0:T(8,128)}, u32[]{:S(2)}) copy-start(f32[96,96]{1,0:T(8,128)} %param.17) | copy-start | bytes 110596
  2.5 0.7 copy-start.9
  5.8 3.3 %copy-start.10 = (f32[2,48,128]{2,1,0:T(8,128)S(1)}, f32[2,48,128]{2,1,0:T(8,128)}, u32[]{:S(2)}) copy-start(f32[2,48,128]{2,1,0:T(8,128)} %param.13) | copy-start | bytes 147460
  5.8 11.9 %collective-permute-start = (bf16[96,2048]{1,0:T(8,128)(2,1)S(1)}, bf16[96,2048]{1,0:T(8,128)(2,1)S(1)}, u32[]{:S(2)}, u32[]{:S(2)}) collective-permute-start(bf16[96,2048]{1,0:T(8,128)(2,1)S(1)} %fusion.8), channel_id=1, source_target_pairs={{0,1},{1,0},{2,3},{3,2},{4,5},{5,4},{6,7},{7,6},{8,9},{9,8},{10,11... | collective-permute-start | bytes 1179656 | tf_op jit(solution)/shard_map/ppermute | solution.py:10
  10.5 0.9 copy-start.4
  11.4 6.3 %copy-start.7 = (f32[2,96,96]{2,1,0:T(8,128)S(1)}, f32[2,96,96]{2,1,0:T(8,128)}, u32[]{:S(2)}) copy-start(f32[2,96,96]{2,1,0:T(8,128)} %param.15) | copy-start | bytes 221188
  62.7 15.0 %copy-start.12 = (f32[48,128]{1,0:T(8,128)S(1)}, f32[48,128]{1,0:T(8,128)}, u32[]{:S(2)}) copy-start(f32[48,128]{1,0:T(8,128)} %param.16) | copy-start | bytes 73732
  62.7 43.0 %all-to-all-start = ((f32[64,96,32]{1,2,0:T(8,128)}), f32[64,96,32]{1,2,0:T(8,128)S(1)}, u32[]{:S(2)}, u32[]{:S(2)}) async-start(f32[64,96,32]{1,2,0:T(8,128)} %constant_dynamic-update-slice_fusion), calls=%async_computation | async-start | bytes 2097152 | tf_op jit(solution)/shard_map/all_to_all | solution.py:67
  78.5 1.1 copy-start.6
  79.7 0.7 copy-start.5
  105.7 1.2 copy-start.2
  107.0 6.6 %copy-start.11 = (f32[64,128]{1,0:T(8,128)S(1)}, f32[64,128]{1,0:T(8,128)}, u32[]{:S(2)}) copy-start(f32[64,128]{1,0:T(8,128)} %param.18) | copy-start | bytes 98308
  107.9 25.5 %collective-permute-start.1 = (bf16[96,2048]{1,0:T(8,128)(2,1)}, bf16[96,2048]{1,0:T(8,128)(2,1)}, u32[]{:S(2)}, u32[]{:S(2)}) collective-permute-start(bf16[96,2048]{1,0:T(8,128)(2,1)} %fusion.6), channel_id=1, source_target_pairs={{0,4},{1,5},{2,6},{3,7},{4,0},{5,1},{6,2},{7,3},{8,12},{9,13},{10,... | collective-permute-start | bytes 1179656 | tf_op jit(solution)/shard_map/ppermute | solution.py:10
  115.6 17.8 %copy-start.8 = (f32[2,96,96]{2,1,0:T(8,128)S(1)}, f32[2,96,96]{2,1,0:T(8,128)}, u32[]{:S(2)}) copy-start(f32[2,96,96]{2,1,0:T(8,128)} %param.15) | copy-start | bytes 221188
  116.5 18.4 %copy-start.3 = (f32[64,48]{0,1:T(8,128)S(1)}, f32[64,48]{0,1:T(8,128)}, u32[]{:S(2)}) copy-start(f32[64,48]{0,1:T(8,128)} %param.19) | copy-start | bytes 36868
  134.9 1.0 copy-start.1
